TPU v7x, 32 devices: a whole 2x2x4 slice. The times are simulated.
32 devices in a mesh: seq: 4 (over x, core), dp: 4 (over z), tensor: 2 (over y).
Axes of the slice: x: 2, y: 2, z: 4, core: 2. Of those that a mesh axis runs over, the one named last changes fastest.
Arguments:
- queries: bfloat16 [4, 1536, 2048], P('dp', ('seq', 'tensor')), may hold values from -128 to 128
- key_vectors: bfloat16 [4, 1536, 2048], P('dp', ('seq', 'tensor')), may hold values from -6 to 6
- values: bfloat16 [4, 1536, 2048], P('dp', ('seq', 'tensor')), may hold values from -6 to 6
- out_grad: bfloat16 [4, 1536, 2048], P('dp', ('seq', 'tensor')), may hold values from -6 to 6
- positions: int32 [4, 1536], P('dp', 'seq'), may hold values from -1 to 8191, as said below
- sink_logits: float32 [16], P('tensor'), may hold values from -1 to 3
Outputs:
- attended: bfloat16 [4, 1536, 2048], P('dp', ('seq', 'tensor'))
- query_grad: bfloat16 [4, 1536, 2048], P('dp', ('seq', 'tensor'))
- key_grad: bfloat16 [4, 1536, 2048], P('dp', ('seq', 'tensor'))
- value_grad: bfloat16 [4, 1536, 2048], P('dp', ('seq', 'tensor'))
- sink_grad: float32 [16], P('tensor')
Inputs may be any that keep to these rules, and one draw needn't show every extreme that they name: Each document's tokens 0 to 8191 form slabs of 4096 tokens; each slab keeps exactly 512 routed tokens, its first half on one sequence shard of 384 slots and its second half on the next. A shard lists its routed positions in rising order in its first slots and -1 in the slots left over; it holds 128 to 384 routed tokens, and some shard of every document holds 384.
All inputs are finite; a program needn't handle non-finite values.
Results may differ from a plain program's by a relative error of at most 0.02.
Values may be sent and summed in bfloat16 or wider, within the bound.
No kernel may reach another device: no remote copies, remote signals or barrier semaphores. Data moves between devices by JAX's collectives and lax.ppermute only.
A program may use at most 128 MiB of HBM per device.

v0:
```python
import functools

import jax
import jax.numpy as jnp
from jax import lax
from jax.experimental import pallas as pl
from jax.experimental.pallas import tpu as pltpu
from jax.sharding import PartitionSpec as P


DH = 128
SCALE = DH ** (-0.5)
NEG = -1e30
LOG2E = 1.4426950408889634
KEEP = 512
QB = 256
CUT = 128
COUNT_ROWS = 16
F32 = jnp.float32
BF16 = jnp.bfloat16
ANY = pl.BlockSpec(memory_space=pl.ANY)
IN_VMEM = pl.BlockSpec(memory_space=pltpu.VMEM)
NT = (((1,), (1,)), ((), ()))
NN = (((1,), (0,)), ((), ()))


def dot(a, b, dims):
    return lax.dot_general(a, b, dims, preferred_element_type=F32)


class Plan:
    def __init__(self, seq, tensor, rows, features):
        self.seq, self.tensor, self.rows = seq, tensor, rows
        self.peers = seq * tensor
        self.slots = rows * self.peers
        self.capacity = rows * tensor
        self.slabs = seq // 2
        self.kept = self.slabs * KEEP
        self.group_heads = features // DH // tensor
        self.heads = self.group_heads // seq

    def where(self):
        return lax.axis_index("seq"), lax.axis_index("tensor")

    def peer(self, k):
        seq_index, tensor_index = self.where()
        return seq_index ^ (k // self.tensor), tensor_index ^ (k % self.tensor)

    def column(self, k, head):
        seq_index, tensor_index = self.peer(k)
        owned = tensor_index * self.group_heads + seq_index * self.heads + head
        return pl.multiple_of(owned * DH, DH)

    def first_row(self, k):
        seq_index, tensor_index = self.peer(k)
        return pl.multiple_of((seq_index * self.tensor + tensor_index) * self.rows, 16)

    def first_count(self, k):
        seq_index, tensor_index = self.peer(k)
        return pl.multiple_of((seq_index * self.tensor + tensor_index) * COUNT_ROWS, 16)


def run_copies(copies):
    for copy in copies:
        copy.start()
    for copy in copies:
        copy.wait()


def pack_kernel(plan, head, *refs):
    arrays, positions = refs[:4], refs[4]
    outs, sem = refs[5:-1], refs[-1]
    rows = plan.rows
    copies = []
    for k in range(plan.peers):
        for at, array in enumerate(arrays):
            copies.append(
                pltpu.make_async_copy(
                    array.at[0, :, pl.ds(plan.column(k, head), DH)],
                    outs[k].at[pl.ds(at * rows, rows), :],
                    sem,
                )
            )
    for copy in copies:
        copy.start()
    _, tensor_index = plan.where()
    slot = lax.broadcasted_iota(jnp.int32, positions.shape, 1) - tensor_index * rows
    filled = (positions[...] >= 0) & (slot >= 0) & (slot < rows)
    count = jnp.sum(filled.astype(F32), axis=1, keepdims=True)
    tile = jnp.broadcast_to(count, (COUNT_ROWS, DH)).astype(BF16)
    for k in range(plan.peers):
        outs[k][4 * rows :, :] = tile
    for copy in copies:
        copy.wait()


def pack(plan, head, arrays, positions):
    out = jax.ShapeDtypeStruct((4 * plan.rows + COUNT_ROWS, DH), BF16)
    return pl.pallas_call(
        functools.partial(pack_kernel, plan, head),
        out_shape=(out,) * plan.peers,
        in_specs=[ANY] * 4 + [IN_VMEM],
        out_specs=(IN_VMEM,) * plan.peers,
        scratch_shapes=[pltpu.SemaphoreType.DMA(())],
    )(*arrays, positions)


def selection(rows, columns, shift, limit=None):
    i = lax.broadcasted_iota(jnp.int32, (rows, columns), 0)
    j = lax.broadcasted_iota(jnp.int32, (rows, columns), 1)
    chosen = j == i + shift
    if limit is not None:
        chosen = chosen & (i < limit)
    return jnp.where(chosen, 1.0, 0.0).astype(BF16)


def compact(plan, slab, first_count, x_ref, y_ref):
    capacity = plan.capacity
    base = slab * KEEP
    here = slab * 2 * capacity
    aligned = pl.multiple_of((first_count // 16) * 16, 16)
    rest = first_count - aligned
    head_part = selection(CUT, CUT, -rest)
    cross_part = selection(CUT, 2 * CUT, CUT - rest)
    row = lax.broadcasted_iota(jnp.int32, (CUT, DH), 0)
    for at in range(4):
        y_ref[at, base : base + capacity, :] = x_ref[at, here : here + capacity, :]
        for part in range(capacity // CUT):
            second = here + capacity + part * CUT
            target = pl.ds(pl.multiple_of(base + aligned + part * CUT, 16), CUT)
            if part == 0:
                moved = dot(head_part, x_ref[at, second : second + CUT, :], NN)
                old = y_ref[at, target, :].astype(F32)
                moved = jnp.where(row < rest, old, moved)
            else:
                moved = dot(cross_part, x_ref[at, second - CUT : second + CUT, :], NN)
            y_ref[at, target, :] = moved.astype(BF16)


def spread(plan, slab, first_count, second_count, r_ref, x_ref):
    capacity = plan.capacity
    base = slab * KEEP
    here = slab * 2 * capacity
    aligned = pl.multiple_of((first_count // 16) * 16, 16)
    rest = first_count - aligned
    row = lax.broadcasted_iota(jnp.int32, (capacity, DH), 0)
    for at in range(4):
        kept = r_ref[at, base : base + capacity, :]
        kept = jnp.where(row < first_count, kept.astype(F32), 0.0).astype(BF16)
        x_ref[at, here : here + capacity, :] = kept
    for part in range(capacity // CUT):
        chosen = selection(CUT, 2 * CUT, rest, second_count - part * CUT)
        source = pl.ds(pl.multiple_of(base + aligned + part * CUT, 16), 2 * CUT)
        target = here + capacity + part * CUT
        for at in range(4):
            moved = dot(chosen, r_ref[at, source, :], NN)
            x_ref[at, target : target + CUT, :] = moved.astype(BF16)


def attention_kernel(plan, head, *refs):
    peers, rows = plan.peers, plan.rows
    sink_ref = refs[0]
    bufs = refs[1 : 1 + peers]
    outs = refs[1 + peers : 1 + 2 * peers]
    sink_out = refs[1 + 2 * peers]
    (x_ref, count_ref, y_ref, kt_ref, vt_ref, s_ref, dk_ref, dv_ref, r_ref, sem) = refs[
        2 + 2 * peers :
    ]
    copies = []
    for k in range(peers):
        first = plan.first_row(k)
        for at in range(4):
            copies.append(
                pltpu.make_async_copy(
                    bufs[k].at[pl.ds(at * rows, rows), :],
                    x_ref.at[at, pl.ds(first, rows), :],
                    sem,
                )
            )
        copies.append(
            pltpu.make_async_copy(
                bufs[k].at[pl.ds(4 * rows, COUNT_ROWS), :],
                count_ref.at[pl.ds(plan.first_count(k), COUNT_ROWS), :],
                sem,
            )
        )
    run_copies(copies)

    shard_counts = []
    for shard in range(plan.seq):
        first = shard * plan.tensor * COUNT_ROWS
        tiles = count_ref[first : first + plan.tensor * COUNT_ROWS, :].astype(F32)
        shard_counts.append((jnp.sum(tiles) * (1.0 / (COUNT_ROWS * DH))).astype(jnp.int32))
    for slab in range(plan.slabs):
        compact(plan, slab, shard_counts[2 * slab], x_ref, y_ref)

    own_seq, _ = plan.where()
    local_head = own_seq * plan.heads + head
    sink = sink_ref[local_head]
    kt_ref[...] = y_ref[1, : plan.kept, :].T
    vt_ref[...] = y_ref[2, : plan.kept, :].T
    behind = lax.broadcasted_iota(jnp.int32, (QB, QB), 0) > lax.broadcasted_iota(
        jnp.int32, (QB, QB), 1
    )
    blocks = plan.kept // QB
    sink_sum = jnp.zeros((1, QB), F32)
    state = {}

    def at_block(b):
        return slice(b * QB, (b + 1) * QB)

    def held(j, b):
        return (j % 2, at_block(b))

    def start(j):
        state[j] = dict(
            q=y_ref[0, at_block(j), :],
            g=y_ref[3, at_block(j), :],
            top=None,
            total=None,
            attended=None,
            query_grad=None,
        )

    def add(now, more):
        return more if now is None else now + more

    def scores(j, b):
        own = state[j]
        s = dot(y_ref[1, at_block(b), :], own["q"], NT)
        if b == j:
            s = jnp.where(behind, NEG, s)
        s_ref[held(j, b)] = s
        top = jnp.max(s.reshape(QB // 8, 8, QB), axis=0)
        own["top"] = top if own["top"] is None else jnp.maximum(own["top"], top)

    def row_max(j):
        own = state[j]
        top = jnp.max(own["top"], axis=0, keepdims=True) * (SCALE * LOG2E)
        own["max"] = jnp.maximum(top, sink * LOG2E)

    def exponentials(j, b):
        own = state[j]
        e = jnp.exp2(s_ref[held(j, b)] * (SCALE * LOG2E) - own["max"])
        s_ref[held(j, b)] = e
        own["total"] = add(own["total"], jnp.sum(e.reshape(QB // 8, 8, QB), axis=0))

    def row_total(j):
        own = state[j]
        own["sink"] = jnp.exp2(sink * LOG2E - own["max"])
        own["inverse"] = 1.0 / (jnp.sum(own["total"], axis=0, keepdims=True) + own["sink"])

    def weigh(j, b):
        own = state[j]
        w = s_ref[held(j, b)] * own["inverse"]
        s_ref[held(j, b)] = w
        half = w.astype(BF16)
        own["attended"] = add(own["attended"], dot(vt_ref[:, at_block(b)], half, NN))
        dv = dot(half, own["g"], NN)
        dv_ref[at_block(b), :] = dv if b == j else dv_ref[at_block(b), :] + dv

    def deltas(j):
        own = state[j]
        attended = own["attended"].astype(BF16)
        r_ref[0, at_block(j), :] = attended.T
        own["delta"] = jnp.sum(
            attended.astype(F32) * own["g"].astype(F32).T, axis=0, keepdims=True
        )
        return own["sink"] * own["inverse"] * own["delta"]

    def gradients(j, b):
        own = state[j]
        dp = dot(y_ref[2, at_block(b), :], own["g"], NT)
        ds = (s_ref[held(j, b)] * (dp - own["delta"])).astype(BF16)
        own["query_grad"] = add(own["query_grad"], dot(kt_ref[:, at_block(b)], ds, NN))
        dk = dot(ds, own["q"], NN)
        dk_ref[at_block(b), :] = dk if b == j else dk_ref[at_block(b), :] + dk

    def finish(j):
        r_ref[1, at_block(j), :] = (state[j]["query_grad"] * SCALE).astype(BF16).T

    for j in range(blocks + 1):
        if j < blocks:
            start(j)
            for b in range(j + 1):
                scores(j, b)
            row_max(j)
        for b in range(j + 1):
            if j < blocks:
                exponentials(j, b)
            if b < j:
                gradients(j - 1, b)
        if j > 0:
            finish(j - 1)
        if j < blocks:
            row_total(j)
            for b in range(j + 1):
                weigh(j, b)
            sink_sum = sink_sum - deltas(j)
    r_ref[2, : plan.kept, :] = (dk_ref[...] * SCALE).astype(BF16)
    r_ref[3, : plan.kept, :] = dv_ref[...].astype(BF16)
    for at in range(4):
        r_ref[at, plan.kept :, :] = jnp.zeros((r_ref.shape[1] - plan.kept, DH), BF16)
    for slab in range(plan.slabs):
        spread(plan, slab, shard_counts[2 * slab], shard_counts[2 * slab + 1], r_ref, x_ref)

    copies = []
    for k in range(peers):
        first = plan.first_row(k)
        for at in range(4):
            copies.append(
                pltpu.make_async_copy(
                    x_ref.at[at, pl.ds(first, rows), :],
                    outs[k].at[pl.ds(at * rows, rows), :],
                    sem,
                )
            )
    for copy in copies:
        copy.start()
    total = jnp.sum(sink_sum, axis=1, keepdims=True)
    row = lax.broadcasted_iota(jnp.int32, sink_out.shape, 0)
    sink_out[...] = jnp.where(row == local_head, total, 0.0)
    for copy in copies:
        copy.wait()


def attention(plan, head, sink_logits, bufs):
    out = jax.ShapeDtypeStruct((4 * plan.rows, DH), BF16)
    kept = plan.kept
    reach = kept - KEEP + 2 * plan.capacity + CUT
    sink_rows = -(-plan.group_heads // 8) * 8
    results = pl.pallas_call(
        functools.partial(attention_kernel, plan, head),
        out_shape=(out,) * plan.peers + (jax.ShapeDtypeStruct((sink_rows, DH), F32),),
        in_specs=[pl.BlockSpec(memory_space=pltpu.SMEM)] + [ANY] * plan.peers,
        out_specs=(ANY,) * plan.peers + (IN_VMEM,),
        scratch_shapes=[
            pltpu.VMEM((4, plan.slots, DH), BF16),
            pltpu.VMEM((plan.peers * COUNT_ROWS, DH), BF16),
            pltpu.VMEM((4, reach, DH), BF16),
            pltpu.VMEM((DH, kept), BF16),
            pltpu.VMEM((DH, kept), BF16),
            pltpu.VMEM((2, kept, QB), F32),
            pltpu.VMEM((kept, DH), F32),
            pltpu.VMEM((kept, DH), F32),
            pltpu.VMEM((4, reach, DH), BF16),
            pltpu.SemaphoreType.DMA(()),
        ],
    )(sink_logits, *bufs)
    return results[:-1], results[-1]


def unpack_kernel(plan, head, carried, *refs):
    bufs = refs[: plan.peers]
    sem = refs[-1]
    outs = refs[plan.peers + (4 if carried else 0) : -1]
    rows = plan.rows
    copies = []
    for k in range(plan.peers):
        for at, out in enumerate(outs):
            copies.append(
                pltpu.make_async_copy(
                    bufs[k].at[pl.ds(at * rows, rows), :],
                    out.at[0, :, pl.ds(plan.column(k, head), DH)],
                    sem,
                )
            )
    run_copies(copies)


def unpack(plan, head, bufs, held, features):
    out = jax.ShapeDtypeStruct((1, plan.rows, features), BF16)
    carried = held is not None
    held = held if carried else ()
    return pl.pallas_call(
        functools.partial(unpack_kernel, plan, head, carried),
        out_shape=(out,) * 4,
        in_specs=[IN_VMEM] * plan.peers + [ANY] * len(held),
        out_specs=(ANY,) * 4,
        scratch_shapes=[pltpu.SemaphoreType.DMA(())],
        input_output_aliases={plan.peers + at: at for at in range(len(held))},
    )(*bufs, *held)


def exchange(plan, bufs):
    axes = ("seq", "tensor")
    swapped = [bufs[0]] * plan.peers
    order = sorted(range(1, plan.peers), key=lambda k: (bin(k).count("1"), -k))
    for k in order:
        pairs = [(i, i ^ k) for i in range(plan.peers)]
        swapped[k] = lax.ppermute(bufs[k], axes, pairs)
    return swapped


def swap_sum(value, axis, step):
    pairs = [(i, i ^ step) for i in range(lax.axis_size(axis))]
    return value + lax.ppermute(value, axis, pairs)


def steps_of(axis):
    size = lax.axis_size(axis)
    return [1 << bit for bit in reversed(range(size.bit_length() - 1))]


def by_heads(queries, key_vectors, values, out_grad, positions, sink_logits):
    seq, tensor = lax.axis_size("seq"), lax.axis_size("tensor")
    rows, features = queries.shape[1:]
    plan = Plan(seq, tensor, rows, features)
    arrays = (queries, key_vectors, values, out_grad)
    received = []
    for head in range(plan.heads):
        received.append(exchange(plan, pack(plan, head, arrays, positions)))
    outs = None
    sink_sum = None
    for head in range(plan.heads):
        last = head == plan.heads - 1
        results, sink_part = attention(plan, head, sink_logits, received[head])
        sink_sum = sink_part if sink_sum is None else sink_sum + sink_part
        if last:
            for axis in ("seq", "dp"):
                for step in steps_of(axis):
                    sink_sum = swap_sum(sink_sum, axis, step)
        results = exchange(plan, results)
        outs = unpack(plan, head, results, outs, features)
    return (*outs, sink_sum[: plan.group_heads, 0])


def block_scores(query_block, query_pos, key_block, key_pos):
    raw_scores = jnp.einsum(
        "ghd,khd->hgk", query_block, key_block, preferred_element_type=jnp.float32
    )
    scores = raw_scores * DH ** (-0.5)
    visible = (key_pos[None, :] <= query_pos[:, None]) & (key_pos[None, :] >= 0)
    return jnp.where(visible[None], scores, -1e30)


def row_stats(query_rows, query_pos, last_slab, key_all, key_pos, sink_logits, key_span):
    head_count = query_rows.shape[1]
    row_count = query_rows.shape[0]
    start_max = jnp.broadcast_to(sink_logits[:, None], (head_count, row_count))
    start_total = jnp.zeros((head_count, row_count), jnp.float32)

    def row_one_block(block, loop_state):
        row_max, row_total = loop_state
        key_block = lax.dynamic_slice_in_dim(key_all, block * key_span, key_span, 0)
        pos_block = lax.dynamic_slice_in_dim(key_pos, block * key_span, key_span, 0)
        scores = block_scores(query_rows, query_pos, key_block, pos_block)
        new_max = jnp.maximum(row_max, jnp.max(scores, axis=2))
        row_total = row_total * jnp.exp(row_max - new_max) + jnp.sum(
            jnp.exp(scores - new_max[:, :, None]), axis=2
        )
        return (new_max, row_total)

    row_max, row_total = lax.fori_loop(0, last_slab + 1, row_one_block, (start_max, start_total))
    return (row_max, row_total + jnp.exp(sink_logits[:, None] - row_max))


def attend_rows(
    query_rows, query_pos, last_slab, key_all, value_all, key_pos, row_max, row_total, key_span
):

    def attend_one_block(block, summed):
        key_block = lax.dynamic_slice_in_dim(key_all, block * key_span, key_span, 0)
        value_block = lax.dynamic_slice_in_dim(value_all, block * key_span, key_span, 0)
        pos_block = lax.dynamic_slice_in_dim(key_pos, block * key_span, key_span, 0)
        scores = block_scores(query_rows, query_pos, key_block, pos_block)
        weights_half = (jnp.exp(scores - row_max[:, :, None]) / row_total[:, :, None]).astype(
            jnp.bfloat16
        )
        return summed + jnp.einsum(
            "hgk,khd->ghd", weights_half, value_block, preferred_element_type=jnp.float32
        )

    summed = lax.fori_loop(
        0, last_slab + 1, attend_one_block, jnp.zeros(query_rows.shape, jnp.float32)
    )
    return summed.astype(jnp.bfloat16)


def query_grads(
    query_rows,
    grad_rows,
    query_pos,
    last_slab,
    key_all,
    value_all,
    key_pos,
    row_max,
    row_total,
    delta_rows,
    key_span,
    key_sums,
    value_sums,
):

    def query_one_block(block, loop_state):
        query_sum, key_state, value_state = loop_state
        key_block = lax.dynamic_slice_in_dim(key_all, block * key_span, key_span, 0)
        value_block = lax.dynamic_slice_in_dim(value_all, block * key_span, key_span, 0)
        pos_block = lax.dynamic_slice_in_dim(key_pos, block * key_span, key_span, 0)
        scores = block_scores(query_rows, query_pos, key_block, pos_block)
        weights_full = jnp.exp(scores - row_max[:, :, None]) / row_total[:, :, None]
        value_dots = jnp.einsum(
            "ghd,khd->hgk", grad_rows, value_block, preferred_element_type=jnp.float32
        )
        score_grad = (weights_full * (value_dots - delta_rows[:, :, None]) * DH ** (-0.5)).astype(
            jnp.bfloat16
        )
        query_sum = query_sum + jnp.einsum(
            "hgk,khd->ghd", score_grad, key_block, preferred_element_type=jnp.float32
        )
        return (query_sum, key_state, value_state)

    start = (jnp.zeros(query_rows.shape, jnp.float32), key_sums, value_sums)
    query_sum, key_sums, value_sums = lax.fori_loop(0, last_slab + 1, query_one_block, start)
    return (query_sum.astype(jnp.bfloat16), key_sums, value_sums)


def key_grads(
    key_rows,
    value_rows,
    key_pos,
    query_all,
    grad_all,
    query_pos_all,
    max_all,
    total_all,
    delta_all,
    first_slab,
    slab_count,
    query_span,
):

    def key_one_block(block, loop_state):
        key_sum, value_sum = loop_state
        query_block = lax.dynamic_slice_in_dim(query_all, block * query_span, query_span, 0)
        grad_block = lax.dynamic_slice_in_dim(grad_all, block * query_span, query_span, 0)
        pos_block = lax.dynamic_slice_in_dim(query_pos_all, block * query_span, query_span, 0)
        max_block = lax.dynamic_slice_in_dim(max_all, block * query_span, query_span, 1)
        total_block = lax.dynamic_slice_in_dim(total_all, block * query_span, query_span, 1)
        delta_block = lax.dynamic_slice_in_dim(delta_all, block * query_span, query_span, 1)
        scores = block_scores(query_block, pos_block, key_rows, key_pos)
        weights_full = jnp.exp(scores - max_block[:, :, None]) / total_block[:, :, None]
        value_dots = jnp.einsum(
            "ghd,khd->hgk", grad_block, value_rows, preferred_element_type=jnp.float32
        )
        score_grad = (weights_full * (value_dots - delta_block[:, :, None]) * DH ** (-0.5)).astype(
            jnp.bfloat16
        )
        key_sum = key_sum + jnp.einsum(
            "hgk,ghd->khd", score_grad, query_block, preferred_element_type=jnp.float32
        )
        value_sum = value_sum + jnp.einsum(
            "hgk,ghd->khd",
            weights_full.astype(jnp.bfloat16),
            grad_block,
            preferred_element_type=jnp.float32,
        )
        return (key_sum, value_sum)

    zeros = jnp.zeros(key_rows.shape, jnp.float32)
    return lax.fori_loop(first_slab, slab_count, key_one_block, (zeros, zeros))


def by_rows(queries, key_vectors, values, out_grad, positions, sink_logits):
    queries, key_vectors, values, out_grad = (
        lax.all_to_all(queries, "tensor", split_axis=2, concat_axis=1, tiled=True),
        lax.all_to_all(key_vectors, "tensor", split_axis=2, concat_axis=1, tiled=True),
        lax.all_to_all(values, "tensor", split_axis=2, concat_axis=1, tiled=True),
        lax.all_to_all(out_grad, "tensor", split_axis=2, concat_axis=1, tiled=True),
    )
    capacity = queries.shape[1]
    features = queries.shape[2]
    head_count = features // DH
    key_span = 2 * capacity
    seq_count = lax.axis_size("seq")
    seq_index = lax.axis_index("seq")
    query_rows = queries[0].reshape(capacity, head_count, DH)
    key_rows = key_vectors[0].reshape(capacity, head_count, DH)
    value_rows = values[0].reshape(capacity, head_count, DH)
    grad_rows = out_grad[0].reshape(capacity, head_count, DH)
    pos_rows = positions[0]
    key_all, value_all, key_pos = (
        lax.all_gather(key_rows, "seq", axis=0, tiled=True),
        lax.all_gather(value_rows, "seq", axis=0, tiled=True),
        lax.all_gather(pos_rows, "seq", axis=0, tiled=True),
    )
    own_slab = seq_index // 2
    groups = (query_rows, grad_rows, pos_rows, own_slab)
    key_sums = None
    value_sums = None
    sink_sum = jnp.zeros((head_count,), jnp.float32)
    group_rows, group_grads, group_pos, last_slab = groups
    row_max, row_total = row_stats(
        group_rows, group_pos, last_slab, key_all, key_pos, sink_logits, key_span
    )
    attended = attend_rows(
        group_rows, group_pos, last_slab, key_all, value_all, key_pos, row_max, row_total, key_span
    )
    delta_rows = jnp.sum(attended.astype(jnp.float32) * group_grads.astype(jnp.float32), axis=2).T
    sink_sum = sink_sum - jnp.sum(
        jnp.exp(sink_logits[:, None] - row_max) / row_total * delta_rows, axis=1
    )
    query_grad, key_sums, value_sums = query_grads(
        group_rows,
        group_grads,
        group_pos,
        last_slab,
        key_all,
        value_all,
        key_pos,
        row_max,
        row_total,
        delta_rows,
        key_span,
        key_sums,
        value_sums,
    )
    results = (attended, query_grad, row_max, row_total, delta_rows)
    attended = results[0]
    query_grad = results[1]
    own_max = results[2]
    own_total = results[3]
    own_delta = results[4]
    query_all, grad_all, query_pos_all = (
        lax.all_gather(query_rows, "seq", axis=0, tiled=True),
        lax.all_gather(grad_rows, "seq", axis=0, tiled=True),
        lax.all_gather(pos_rows, "seq", axis=0, tiled=True),
    )
    max_all, total_all, delta_all = (
        lax.all_gather(own_max, "seq", axis=1, tiled=True),
        lax.all_gather(own_total, "seq", axis=1, tiled=True),
        lax.all_gather(own_delta, "seq", axis=1, tiled=True),
    )
    key_sum, value_sum = key_grads(
        key_rows,
        value_rows,
        pos_rows,
        query_all,
        grad_all,
        query_pos_all,
        max_all,
        total_all,
        delta_all,
        own_slab,
        seq_count // 2,
        key_span,
    )
    key_grad, value_grad = (
        lax.all_to_all(
            key_sum.astype(jnp.bfloat16).reshape(1, capacity, features),
            "tensor",
            split_axis=1,
            concat_axis=2,
            tiled=True,
        ),
        lax.all_to_all(
            value_sum.astype(jnp.bfloat16).reshape(1, capacity, features),
            "tensor",
            split_axis=1,
            concat_axis=2,
            tiled=True,
        ),
    )
    attended, query_grad = (
        lax.all_to_all(
            attended.reshape(1, capacity, features),
            "tensor",
            split_axis=1,
            concat_axis=2,
            tiled=True,
        ),
        lax.all_to_all(
            query_grad.reshape(1, capacity, features),
            "tensor",
            split_axis=1,
            concat_axis=2,
            tiled=True,
        ),
    )
    sink_grad = lax.psum(sink_sum, ("seq", "dp"))
    return (attended, query_grad, key_grad, value_grad, sink_grad)


def solution(mesh):
    placed = (
        P("dp", ("seq", "tensor"), None),
        P("dp", ("seq", "tensor"), None),
        P("dp", ("seq", "tensor"), None),
        P("dp", ("seq", "tensor"), None),
        P("dp", "seq"),
        P("tensor"),
    )
    sizes = (mesh.shape["seq"], mesh.shape["tensor"], mesh.shape["dp"])

    def on_device(queries, *rest):
        heads = queries.shape[2] // DH
        even = all(size & (size - 1) == 0 for size in sizes)
        rows = queries.shape[1]
        capacity = rows * sizes[1]
        aligned = rows % 16 == 0 and rows <= 256 and capacity % CUT == 0
        aligned = aligned and sizes[0] > 1 and capacity < KEEP <= 4 * capacity // 3
        if even and aligned and heads % (sizes[0] * sizes[1]) == 0:
            return by_heads(queries, *rest)
        return by_rows(queries, *rest)

    return jax.shard_map(
        on_device,
        mesh=mesh,
        in_specs=placed,
        out_specs=(
            P("dp", ("seq", "tensor"), None),
            P("dp", ("seq", "tensor"), None),
            P("dp", ("seq", "tensor"), None),
            P("dp", ("seq", "tensor"), None),
            P("tensor"),
        ),
        check_vma=False,
    )
```

profile of v0, /device:TPU:0, one launch (start us, length us, event | category | flops | bytes accessed | tf_op | source)
XLA Modules:
  0.0 104.4 jit_solution(4283697314673106900)
XLA Ops:
  0.6 3.3 %shard_map.103 = (bf16[784,128]{1,0:T(8,128)(2,1)}, bf16[784,128]{1,0:T(8,128)(2,1)}, bf16[784,128]{1,0:T(8,128)(2,1)}, bf16[784,128]{1,0:T(8,128)(2,1)}, bf16[7...) custom-call(bf16[1,192,2048]{2,1,0:T(8,128)(2,1)} %refs_0_.6, ...), custom_call_target="tpu_custom_call" | custom-call | tf_op jit(solution)/shard_map/pallas_call | solution.py:99
  3.9 3.1 %collective-permute-start.14 = (bf16[784,128]{1,0:T(8,128)(2,1)}, bf16[784,128]{1,0:T(8,128)(2,1)S(1)}, u32[]{:S(2)}, u32[]{:S(2)}) collective-permute-start(bf16[784,128]{1,0:T(8,128)(2,1)} %get-tuple-element.64), channel_id=1, source_target_pairs={{0,1},{1,0},{8,9},{9,8},{16,17},{17,16},{24,25},{25,24},{2,3},{3,2... | collective-permute-start | bytes 602120 | tf_op jit(solution)/shard_map/ppermute | solution.py:391
  7.2 1.9 %collective-permute-start.17 = (bf16[784,128]{1,0:T(8,128)(2,1)}, bf16[784,128]{1,0:T(8,128)(2,1)S(1)}, u32[]{:S(2)}, u32[]{:S(2)}) collective-permute-start(bf16[784,128]{1,0:T(8,128)(2,1)} %get-tuple-element.67), channel_id=1, source_target_pairs={{0,16},{1,17},{8,24},{9,25},{16,0},{17,1},{24,8},{25,9},{2,18},{3,... | collective-permute-start | bytes 602120 | tf_op jit(solution)/shard_map/ppermute | solution.py:391
  10.6 3.2 %shard_map.101 = (bf16[784,128]{1,0:T(8,128)(2,1)}, bf16[784,128]{1,0:T(8,128)(2,1)}, bf16[784,128]{1,0:T(8,128)(2,1)}, bf16[784,128]{1,0:T(8,128)(2,1)}, bf16[7...) custom-call(bf16[1,192,2048]{2,1,0:T(8,128)(2,1)} %refs_0_.6, ...), custom_call_target="tpu_custom_call" | custom-call | tf_op jit(solution)/shard_map/pallas_call | solution.py:99
  14.5 1.8 %collective-permute-start.20 = (bf16[784,128]{1,0:T(8,128)(2,1)S(1)}, bf16[784,128]{1,0:T(8,128)(2,1)S(1)}, u32[]{:S(2)}, u32[]{:S(2)}) collective-permute-start(bf16[784,128]{1,0:T(8,128)(2,1)S(1)} %copy-done.29), channel_id=1, source_target_pairs={{0,25},{1,24},{8,17},{9,16},{16,9},{17,8},{24,1},{25,0},{2,27},{3,... | collective-permute-start | bytes 602120 | tf_op jit(solution)/shard_map/ppermute | solution.py:391
  16.3 3.8 %collective-permute-done.16.refs_4_ = bf16[784,128]{1,0:T(8,128)(2,1)S(1)} collective-permute-done((bf16[784,128]{1,0:T(8,128)(2,1)}, bf16[784,128]{1,0:T(8,128)(2,1)S(1)}, u32[]{:S(2)}, u32[]{:S(2)}) %collective-permute-start.16) | collective-permute-done | bytes 200736 | tf_op jit(solution)/shard_map/ppermute | solution.py:391
  24.0 3.7 %collective-permute-done.20.refs_8_ = bf16[784,128]{1,0:T(8,128)(2,1)S(1)} collective-permute-done((bf16[784,128]{1,0:T(8,128)(2,1)S(1)}, bf16[784,128]{1,0:T(8,128)(2,1)S(1)}, u32[]{:S(2)}, u32[]{:S(2)}) %collective-permute-start.20) | collective-permute-done | bytes 200736 | tf_op jit(solution)/shard_map/ppermute | solution.py:391
  29.2 3.0 %collective-permute-done.refs_2_ = bf16[784,128]{1,0:T(8,128)(2,1)S(1)} collective-permute-done((bf16[784,128]{1,0:T(8,128)(2,1)}, bf16[784,128]{1,0:T(8,128)(2,1)S(1)}, u32[]{:S(2)}, u32[]{:S(2)}) %collective-permute-start) | collective-permute-done | bytes 200736 | tf_op jit(solution)/shard_map/ppermute | solution.py:391
  34.2 8.5 %shard_map.104 = (bf16[768,128]{1,0:T(8,128)(2,1)}, bf16[768,128]{1,0:T(8,128)(2,1)}, bf16[768,128]{1,0:T(8,128)(2,1)}, bf16[768,128]{1,0:T(8,128)(2,1)}, bf16[7...) custom-call(f32[8]{0:T(128)} %refs_0_.7, ...), custom_call_target="tpu_custom_call" | custom-call | tf_op jit(solution)/shard_map/pallas_call | solution.py:332
  47.0 8.6 %shard_map.102 = (bf16[768,128]{1,0:T(8,128)(2,1)}, bf16[768,128]{1,0:T(8,128)(2,1)}, bf16[768,128]{1,0:T(8,128)(2,1)}, bf16[768,128]{1,0:T(8,128)(2,1)}, bf16[7...) custom-call(f32[8]{0:T(128)} %refs_0_.7, ...), custom_call_target="tpu_custom_call" | custom-call | tf_op jit(solution)/shard_map/pallas_call | solution.py:332
  57.1 2.9 %collective-permute-done.28 = f32[8,128]{1,0:T(8,128)S(1)} collective-permute-done((f32[8,128]{1,0:T(8,128)S(1)}, f32[8,128]{1,0:T(8,128)S(1)}, u32[]{:S(2)}, u32[]{:S(2)}) %collective-permute-start.28) | collective-permute-done | bytes 4128 | tf_op jit(solution)/shard_map/ppermute | solution.py:397
  61.1 2.6 %collective-permute-start.30 = (f32[8,128]{1,0:T(8,128)S(1)}, f32[8,128]{1,0:T(8,128)S(1)}, u32[]{:S(2)}, u32[]{:S(2)}) collective-permute-start(f32[8,128]{1,0:T(8,128)S(1)} %add.17), channel_id=1, source_target_pairs={{0,4},{2,6},{4,0},{6,2},{1,5},{3,7},{5,1},{7,3},{8,12},{10,14},{12... | collective-permute-start | bytes 12296 | tf_op jit(solution)/shard_map/ppermute | solution.py:397
  63.7 1.9 %collective-permute-done.30 = f32[8,128]{1,0:T(8,128)S(1)} collective-permute-done((f32[8,128]{1,0:T(8,128)S(1)}, f32[8,128]{1,0:T(8,128)S(1)}, u32[]{:S(2)}, u32[]{:S(2)}) %collective-permute-start.30) | collective-permute-done | bytes 4128 | tf_op jit(solution)/shard_map/ppermute | solution.py:397
  65.6 1.6 %collective-permute-start.31 = (f32[8,128]{1,0:T(8,128)S(1)}, f32[8,128]{1,0:T(8,128)S(1)}, u32[]{:S(2)}, u32[]{:S(2)}) collective-permute-start(f32[8,128]{1,0:T(8,128)S(1)} %add.18), channel_id=1, source_target_pairs={{0,2},{2,0},{4,6},{6,4},{1,3},{3,1},{5,7},{7,5},{8,10},{10,8},{12,... | collective-permute-start | bytes 12296 | tf_op jit(solution)/shard_map/ppermute | solution.py:397
  67.2 2.0 %collective-permute-done.31 = f32[8,128]{1,0:T(8,128)S(1)} collective-permute-done((f32[8,128]{1,0:T(8,128)S(1)}, f32[8,128]{1,0:T(8,128)S(1)}, u32[]{:S(2)}, u32[]{:S(2)}) %collective-permute-start.31) | collective-permute-done | bytes 4128 | tf_op jit(solution)/shard_map/ppermute | solution.py:397
  70.7 2.0 %collective-permute-start.27 = (bf16[768,128]{1,0:T(8,128)(2,1)S(1)}, bf16[768,128]{1,0:T(8,128)(2,1)S(1)}, u32[]{:S(2)}, u32[]{:S(2)}) collective-permute-start(bf16[768,128]{1,0:T(8,128)(2,1)S(1)} %copy-done.31), channel_id=1, source_target_pairs={{0,25},{1,24},{8,17},{9,16},{16,9},{17,8},{24,1},{25,0},{2,27},{3,... | collective-permute-start | bytes 589832 | tf_op jit(solution)/shard_map/ppermute | solution.py:391
  74.0 3.7 %collective-permute-done.25.refs_5_ = bf16[768,128]{1,0:T(8,128)(2,1)S(1)} collective-permute-done((bf16[768,128]{1,0:T(8,128)(2,1)S(1)}, bf16[768,128]{1,0:T(8,128)(2,1)S(1)}, u32[]{:S(2)}, u32[]{:S(2)}) %collective-permute-start.25) | collective-permute-done | bytes 196640 | tf_op jit(solution)/shard_map/ppermute | solution.py:391
  79.1 2.5 %collective-permute-start.10 = (bf16[768,128]{1,0:T(8,128)(2,1)}, bf16[768,128]{1,0:T(8,128)(2,1)S(1)}, u32[]{:S(2)}, u32[]{:S(2)}) collective-permute-start(bf16[768,128]{1,0:T(8,128)(2,1)} %get-tuple-element.59), channel_id=1, source_target_pairs={{0,16},{1,17},{8,24},{9,25},{16,0},{17,1},{24,8},{25,9},{2,18},{3,... | collective-permute-start | bytes 589832 | tf_op jit(solution)/shard_map/ppermute | solution.py:391
  82.5 2.1 %collective-permute-start.11 = (bf16[768,128]{1,0:T(8,128)(2,1)}, bf16[768,128]{1,0:T(8,128)(2,1)S(1)}, u32[]{:S(2)}, u32[]{:S(2)}) collective-permute-start(bf16[768,128]{1,0:T(8,128)(2,1)} %get-tuple-element.60), channel_id=1, source_target_pairs={{0,17},{1,16},{8,25},{9,24},{16,1},{17,0},{24,9},{25,8},{2,19},{3,... | collective-permute-start | bytes 589832 | tf_op jit(solution)/shard_map/ppermute | solution.py:391
  86.4 1.8 %collective-permute-start.13 = (bf16[768,128]{1,0:T(8,128)(2,1)}, bf16[768,128]{1,0:T(8,128)(2,1)S(1)}, u32[]{:S(2)}, u32[]{:S(2)}) collective-permute-start(bf16[768,128]{1,0:T(8,128)(2,1)} %get-tuple-element.62), channel_id=1, source_target_pairs={{0,25},{1,24},{8,17},{9,16},{16,9},{17,8},{24,1},{25,0},{2,27},{3,... | collective-permute-start | bytes 589832 | tf_op jit(solution)/shard_map/ppermute | solution.py:391
  88.8 2.6 %shard_map.105 = (bf16[1,192,2048]{2,1,0:T(8,128)(2,1)}, bf16[1,192,2048]{2,1,0:T(8,128)(2,1)}, bf16[1,192,2048]{2,1,0:T(8,128)(2,1)}, bf16[1,192,2048]{2,1,0:T(8,128)(2,1)}) custom-call(bf16[768,128]{1,0:T(8,128)(2,1)} %get-tuple-element.71.refs_0_, bf16[768,128]{1,0:T(8,128)(2,1)} %copy-done.21, bf16[768,128]{1,0:T(8,128)(2,1)} %copy-done.22, ...), custom_call_target="tpu_custom_call" | custom-call | tf_op jit(solution)/shard_map/pallas_call | solution.py:375
  92.3 5.4 %collective-permute-done.12.refs_6_ = bf16[768,128]{1,0:T(8,128)(2,1)S(1)} collective-permute-done((bf16[768,128]{1,0:T(8,128)(2,1)}, bf16[768,128]{1,0:T(8,128)(2,1)S(1)}, u32[]{:S(2)}, u32[]{:S(2)}) %collective-permute-start.12) | collective-permute-done | bytes 196640 | tf_op jit(solution)/shard_map/ppermute | solution.py:391
  97.7 3.5 %collective-permute-done.13.refs_7_ = bf16[768,128]{1,0:T(8,128)(2,1)S(1)} collective-permute-done((bf16[768,128]{1,0:T(8,128)(2,1)}, bf16[768,128]{1,0:T(8,128)(2,1)S(1)}, u32[]{:S(2)}, u32[]{:S(2)}) %collective-permute-start.13) | collective-permute-done | bytes 196640 | tf_op jit(solution)/shard_map/ppermute | solution.py:391
  101.9 2.6 %shard_map.106 = (bf16[1,192,2048]{2,1,0:T(8,128)(2,1)}, bf16[1,192,2048]{2,1,0:T(8,128)(2,1)}, bf16[1,192,2048]{2,1,0:T(8,128)(2,1)}, bf16[1,192,2048]{2,1,0:T(8,128)(2,1)}) custom-call(bf16[768,128]{1,0:T(8,128)(2,1)} %get-tuple-element.55.refs_0_, ...), custom_call_target="tpu_custom_call", output_to_operand_aliasing={{0}: (8, {}), {1}: (9, {}), {2}: (10, {}), {3}: (11, {})} | custom-call | tf_op jit(solution)/shard_map/pallas_call | solution.py:375
  (120 shorter events, 25.4 us)
Async XLA Ops:
  3.9 9.9 %collective-permute-start.14 = (bf16[784,128]{1,0:T(8,128)(2,1)}, bf16[784,128]{1,0:T(8,128)(2,1)S(1)}, u32[]{:S(2)}, u32[]{:S(2)}) collective-permute-start(bf16[784,128]{1,0:T(8,128)(2,1)} %get-tuple-element.64), channel_id=1, source_target_pairs={{0,1},{1,0},{8,9},{9,8},{16,17},{17,16},{24,25},{25,24},{2,3},{3,2... | collective-permute-start | bytes 602120 | tf_op jit(solution)/shard_map/ppermute | solution.py:391
  7.0 13.2 %collective-permute-start.16 = (bf16[784,128]{1,0:T(8,128)(2,1)}, bf16[784,128]{1,0:T(8,128)(2,1)S(1)}, u32[]{:S(2)}, u32[]{:S(2)}) collective-permute-start(bf16[784,128]{1,0:T(8,128)(2,1)} %get-tuple-element.66), channel_id=1, source_target_pairs={{0,9},{1,8},{8,1},{9,0},{16,25},{17,24},{24,17},{25,16},{2,11},{3,... | collective-permute-start | bytes 602120 | tf_op jit(solution)/shard_map/ppermute | solution.py:391
  7.2 14.2 %collective-permute-start.17 = (bf16[784,128]{1,0:T(8,128)(2,1)}, bf16[784,128]{1,0:T(8,128)(2,1)S(1)}, u32[]{:S(2)}, u32[]{:S(2)}) collective-permute-start(bf16[784,128]{1,0:T(8,128)(2,1)} %get-tuple-element.67), channel_id=1, source_target_pairs={{0,16},{1,17},{8,24},{9,25},{16,0},{17,1},{24,8},{25,9},{2,18},{3,... | collective-permute-start | bytes 602120 | tf_op jit(solution)/shard_map/ppermute | solution.py:391
  9.1 13.3 %collective-permute-start.18 = (bf16[784,128]{1,0:T(8,128)(2,1)}, bf16[784,128]{1,0:T(8,128)(2,1)S(1)}, u32[]{:S(2)}, u32[]{:S(2)}) collective-permute-start(bf16[784,128]{1,0:T(8,128)(2,1)} %get-tuple-element.68), channel_id=1, source_target_pairs={{0,17},{1,16},{8,25},{9,24},{16,1},{17,0},{24,9},{25,8},{2,19},{3,... | collective-permute-start | bytes 602120 | tf_op jit(solution)/shard_map/ppermute | solution.py:391
  14.5 13.3 %collective-permute-start.20 = (bf16[784,128]{1,0:T(8,128)(2,1)S(1)}, bf16[784,128]{1,0:T(8,128)(2,1)S(1)}, u32[]{:S(2)}, u32[]{:S(2)}) collective-permute-start(bf16[784,128]{1,0:T(8,128)(2,1)S(1)} %copy-done.29), channel_id=1, source_target_pairs={{0,25},{1,24},{8,17},{9,16},{16,9},{17,8},{24,1},{25,0},{2,27},{3,... | collective-permute-start | bytes 602120 | tf_op jit(solution)/shard_map/ppermute | solution.py:391
  20.1 12.1 %collective-permute-start = (bf16[784,128]{1,0:T(8,128)(2,1)}, bf16[784,128]{1,0:T(8,128)(2,1)S(1)}, u32[]{:S(2)}, u32[]{:S(2)}) collective-permute-start(bf16[784,128]{1,0:T(8,128)(2,1)} %get-tuple-element.48), channel_id=1, source_target_pairs={{0,1},{1,0},{8,9},{9,8},{16,17},{17,16},{24,25},{25,24},{2,3},{3,2... | collective-permute-start | bytes 602120 | tf_op jit(solution)/shard_map/ppermute | solution.py:391
  21.4 12.1 %collective-permute-start.1 = (bf16[784,128]{1,0:T(8,128)(2,1)}, bf16[784,128]{1,0:T(8,128)(2,1)S(1)}, u32[]{:S(2)}, u32[]{:S(2)}) collective-permute-start(bf16[784,128]{1,0:T(8,128)(2,1)} %get-tuple-element.49), channel_id=1, source_target_pairs={{0,8},{1,9},{8,0},{9,1},{16,24},{17,25},{24,16},{25,17},{2,10},{3,... | collective-permute-start | bytes 602120 | tf_op jit(solution)/shard_map/ppermute | solution.py:391
  22.3 20.4 %collective-permute-start.2 = (bf16[784,128]{1,0:T(8,128)(2,1)}, bf16[784,128]{1,0:T(8,128)(2,1)S(1)}, u32[]{:S(2)}, u32[]{:S(2)}) collective-permute-start(bf16[784,128]{1,0:T(8,128)(2,1)} %get-tuple-element.50), channel_id=1, source_target_pairs={{0,9},{1,8},{8,1},{9,0},{16,25},{17,24},{24,17},{25,16},{2,11},{3,... | collective-permute-start | bytes 602120 | tf_op jit(solution)/shard_map/ppermute | solution.py:391
  23.3 20.8 %collective-permute-start.3 = (bf16[784,128]{1,0:T(8,128)(2,1)}, bf16[784,128]{1,0:T(8,128)(2,1)S(1)}, u32[]{:S(2)}, u32[]{:S(2)}) collective-permute-start(bf16[784,128]{1,0:T(8,128)(2,1)} %get-tuple-element.51), channel_id=1, source_target_pairs={{0,16},{1,17},{8,24},{9,25},{16,0},{17,1},{24,8},{25,9},{2,18},{3,... | collective-permute-start | bytes 602120 | tf_op jit(solution)/shard_map/ppermute | solution.py:391
  27.7 16.4 %collective-permute-start.4 = (bf16[784,128]{1,0:T(8,128)(2,1)}, bf16[784,128]{1,0:T(8,128)(2,1)S(1)}, u32[]{:S(2)}, u32[]{:S(2)}) collective-permute-start(bf16[784,128]{1,0:T(8,128)(2,1)} %get-tuple-element.52), channel_id=1, source_target_pairs={{0,17},{1,16},{8,25},{9,24},{16,1},{17,0},{24,9},{25,8},{2,19},{3,... | collective-permute-start | bytes 602120 | tf_op jit(solution)/shard_map/ppermute | solution.py:391
  32.2 12.8 %collective-permute-start.5 = (bf16[784,128]{1,0:T(8,128)(2,1)}, bf16[784,128]{1,0:T(8,128)(2,1)S(1)}, u32[]{:S(2)}, u32[]{:S(2)}) collective-permute-start(bf16[784,128]{1,0:T(8,128)(2,1)} %get-tuple-element.53), channel_id=1, source_target_pairs={{0,24},{1,25},{8,16},{9,17},{16,8},{17,9},{24,0},{25,1},{2,26},{3,... | collective-permute-start | bytes 602120 | tf_op jit(solution)/shard_map/ppermute | solution.py:391
  33.4 12.9 %collective-permute-start.6 = (bf16[784,128]{1,0:T(8,128)(2,1)}, bf16[784,128]{1,0:T(8,128)(2,1)S(1)}, u32[]{:S(2)}, u32[]{:S(2)}) collective-permute-start(bf16[784,128]{1,0:T(8,128)(2,1)} %get-tuple-element.54), channel_id=1, source_target_pairs={{0,25},{1,24},{8,17},{9,16},{16,9},{17,8},{24,1},{25,0},{2,27},{3,... | collective-permute-start | bytes 602120 | tf_op jit(solution)/shard_map/ppermute | solution.py:391
  42.8 27.8 %collective-permute-start.21 = (bf16[768,128]{1,0:T(8,128)(2,1)}, bf16[768,128]{1,0:T(8,128)(2,1)S(1)}, u32[]{:S(2)}, u32[]{:S(2)}) collective-permute-start(bf16[768,128]{1,0:T(8,128)(2,1)} %get-tuple-element.72), channel_id=1, source_target_pairs={{0,1},{1,0},{8,9},{9,8},{16,17},{17,16},{24,25},{25,24},{2,3},{3,2... | collective-permute-start | bytes 589832 | tf_op jit(solution)/shard_map/ppermute | solution.py:391
  44.1 26.6 %collective-permute-start.22 = (bf16[768,128]{1,0:T(8,128)(2,1)}, bf16[768,128]{1,0:T(8,128)(2,1)S(1)}, u32[]{:S(2)}, u32[]{:S(2)}) collective-permute-start(bf16[768,128]{1,0:T(8,128)(2,1)} %get-tuple-element.73), channel_id=1, source_target_pairs={{0,8},{1,9},{8,0},{9,1},{16,24},{17,25},{24,16},{25,17},{2,10},{3,... | collective-permute-start | bytes 589832 | tf_op jit(solution)/shard_map/ppermute | solution.py:391
  44.1 28.7 %collective-permute-start.23 = (bf16[768,128]{1,0:T(8,128)(2,1)}, bf16[768,128]{1,0:T(8,128)(2,1)S(1)}, u32[]{:S(2)}, u32[]{:S(2)}) collective-permute-start(bf16[768,128]{1,0:T(8,128)(2,1)} %get-tuple-element.74), channel_id=1, source_target_pairs={{0,9},{1,8},{8,1},{9,0},{16,25},{17,24},{24,17},{25,16},{2,11},{3,... | collective-permute-start | bytes 589832 | tf_op jit(solution)/shard_map/ppermute | solution.py:391
  45.0 28.9 %collective-permute-start.24 = (bf16[768,128]{1,0:T(8,128)(2,1)}, bf16[768,128]{1,0:T(8,128)(2,1)S(1)}, u32[]{:S(2)}, u32[]{:S(2)}) collective-permute-start(bf16[768,128]{1,0:T(8,128)(2,1)} %get-tuple-element.75), channel_id=1, source_target_pairs={{0,16},{1,17},{8,24},{9,25},{16,0},{17,1},{24,8},{25,9},{2,18},{3,... | collective-permute-start | bytes 589832 | tf_op jit(solution)/shard_map/ppermute | solution.py:391
  70.7 11.7 %collective-permute-start.27 = (bf16[768,128]{1,0:T(8,128)(2,1)S(1)}, bf16[768,128]{1,0:T(8,128)(2,1)S(1)}, u32[]{:S(2)}, u32[]{:S(2)}) collective-permute-start(bf16[768,128]{1,0:T(8,128)(2,1)S(1)} %copy-done.31), channel_id=1, source_target_pairs={{0,25},{1,24},{8,17},{9,16},{16,9},{17,8},{24,1},{25,0},{2,27},{3,... | collective-permute-start | bytes 589832 | tf_op jit(solution)/shard_map/ppermute | solution.py:391
  72.8 12.8 %collective-permute-start.7 = (bf16[768,128]{1,0:T(8,128)(2,1)}, bf16[768,128]{1,0:T(8,128)(2,1)S(1)}, u32[]{:S(2)}, u32[]{:S(2)}) collective-permute-start(bf16[768,128]{1,0:T(8,128)(2,1)} %get-tuple-element.56), channel_id=1, source_target_pairs={{0,1},{1,0},{8,9},{9,8},{16,17},{17,16},{24,25},{25,24},{2,3},{3,2... | collective-permute-start | bytes 589832 | tf_op jit(solution)/shard_map/ppermute | solution.py:391
  74.0 12.4 %collective-permute-start.8 = (bf16[768,128]{1,0:T(8,128)(2,1)}, bf16[768,128]{1,0:T(8,128)(2,1)S(1)}, u32[]{:S(2)}, u32[]{:S(2)}) collective-permute-start(bf16[768,128]{1,0:T(8,128)(2,1)} %get-tuple-element.57), channel_id=1, source_target_pairs={{0,8},{1,9},{8,0},{9,1},{16,24},{17,25},{24,16},{25,17},{2,10},{3,... | collective-permute-start | bytes 589832 | tf_op jit(solution)/shard_map/ppermute | solution.py:391
  77.7 14.6 %collective-permute-start.9 = (bf16[768,128]{1,0:T(8,128)(2,1)}, bf16[768,128]{1,0:T(8,128)(2,1)S(1)}, u32[]{:S(2)}, u32[]{:S(2)}) collective-permute-start(bf16[768,128]{1,0:T(8,128)(2,1)} %get-tuple-element.58), channel_id=1, source_target_pairs={{0,9},{1,8},{8,1},{9,0},{16,25},{17,24},{24,17},{25,16},{2,11},{3,... | collective-permute-start | bytes 589832 | tf_op jit(solution)/shard_map/ppermute | solution.py:391
  79.1 13.1 %collective-permute-start.10 = (bf16[768,128]{1,0:T(8,128)(2,1)}, bf16[768,128]{1,0:T(8,128)(2,1)S(1)}, u32[]{:S(2)}, u32[]{:S(2)}) collective-permute-start(bf16[768,128]{1,0:T(8,128)(2,1)} %get-tuple-element.59), channel_id=1, source_target_pairs={{0,16},{1,17},{8,24},{9,25},{16,0},{17,1},{24,8},{25,9},{2,18},{3,... | collective-permute-start | bytes 589832 | tf_op jit(solution)/shard_map/ppermute | solution.py:391
  82.5 9.8 %collective-permute-start.11 = (bf16[768,128]{1,0:T(8,128)(2,1)}, bf16[768,128]{1,0:T(8,128)(2,1)S(1)}, u32[]{:S(2)}, u32[]{:S(2)}) collective-permute-start(bf16[768,128]{1,0:T(8,128)(2,1)} %get-tuple-element.60), channel_id=1, source_target_pairs={{0,17},{1,16},{8,25},{9,24},{16,1},{17,0},{24,9},{25,8},{2,19},{3,... | collective-permute-start | bytes 589832 | tf_op jit(solution)/shard_map/ppermute | solution.py:391
  85.5 12.1 %collective-permute-start.12 = (bf16[768,128]{1,0:T(8,128)(2,1)}, bf16[768,128]{1,0:T(8,128)(2,1)S(1)}, u32[]{:S(2)}, u32[]{:S(2)}) collective-permute-start(bf16[768,128]{1,0:T(8,128)(2,1)} %get-tuple-element.61), channel_id=1, source_target_pairs={{0,24},{1,25},{8,16},{9,17},{16,8},{17,9},{24,0},{25,1},{2,26},{3,... | collective-permute-start | bytes 589832 | tf_op jit(solution)/shard_map/ppermute | solution.py:391
  86.4 14.8 %collective-permute-start.13 = (bf16[768,128]{1,0:T(8,128)(2,1)}, bf16[768,128]{1,0:T(8,128)(2,1)S(1)}, u32[]{:S(2)}, u32[]{:S(2)}) collective-permute-start(bf16[768,128]{1,0:T(8,128)(2,1)} %get-tuple-element.62), channel_id=1, source_target_pairs={{0,25},{1,24},{8,17},{9,16},{16,9},{17,8},{24,1},{25,0},{2,27},{3,... | collective-permute-start | bytes 589832 | tf_op jit(solution)/shard_map/ppermute | solution.py:391
  (42 other events, 397.5 us)
where the time goes:
time: 105 us; the launch traced here: 104 us
  waiting for transfers between devices  36.2 us (34%)
  starting transfers between devices  35.8 us (34%)
  Pallas kernels  28.8 us (27%)
  local copies, waits for them, and re-layouts  2.07 us (2%)
    ppermute x28, starting transfers between devices, exchange(): swapped[k] = lax.ppermute(bufs[k], axes, pairs)  30.9 us
    ppermute x28, waiting for transfers between devices, exchange(): swapped[k] = lax.ppermute(bufs[k], axes, pairs)  28.2 us
    pallas_call x2, Pallas kernels, attention(): pl.pallas_call(functools.partial(attention_kernel, plan, head), out_shape...  17.1 us
    ppermute x4, waiting for transfers between devices, swap_sum(): return value + lax.ppermute(value, axis, pairs)  7.97 us
    pallas_call x2, Pallas kernels, pack(): pl.pallas_call(functools.partial(pack_kernel, plan, head), out_shape=(out...  6.5 us
    pallas_call x2, Pallas kernels, unpack(): pl.pallas_call(functools.partial(unpack_kernel, plan, head, carried), out...  5.15 us
    ppermute x4, starting transfers between devices, swap_sum(): return value + lax.ppermute(value, axis, pairs)  4.91 us
  transfers between devices with their start and end apart: 32, of which 15 were waited for; matrix products, arithmetic and copies ran while one was open for 1% of the time, Pallas kernels for 22%

commit v1 on v0

--- a/solution.py
+++ b/solution.py
@@ -19,6 +19,7 @@
 F32 = jnp.float32
 BF16 = jnp.bfloat16
 ANY = pl.BlockSpec(memory_space=pl.ANY)
+IN_HBM = pl.BlockSpec(memory_space=pltpu.HBM)
 IN_VMEM = pl.BlockSpec(memory_space=pltpu.VMEM)
 NT = (((1,), (1,)), ((), ()))
 NN = (((1,), (0,)), ((), ()))
@@ -68,9 +69,11 @@
 
 
 def pack_kernel(plan, head, *refs):
-    arrays, positions = refs[:4], refs[4]
-    outs, sem = refs[5:-1], refs[-1]
+    arrays, positions_hbm = refs[:4], refs[4]
+    outs, positions, sem, positions_sem = refs[5:-3], refs[-3], refs[-2], refs[-1]
     rows = plan.rows
+    fetch = pltpu.make_async_copy(positions_hbm, positions, positions_sem)
+    fetch.start()
     copies = []
     for k in range(plan.peers):
         for at, array in enumerate(arrays):
@@ -85,6 +88,7 @@
         copy.start()
     _, tensor_index = plan.where()
     slot = lax.broadcasted_iota(jnp.int32, positions.shape, 1) - tensor_index * rows
+    fetch.wait()
     filled = (positions[...] >= 0) & (slot >= 0) & (slot < rows)
     count = jnp.sum(filled.astype(F32), axis=1, keepdims=True)
     tile = jnp.broadcast_to(count, (COUNT_ROWS, DH)).astype(BF16)
@@ -99,10 +103,15 @@
     return pl.pallas_call(
         functools.partial(pack_kernel, plan, head),
         out_shape=(out,) * plan.peers,
-        in_specs=[ANY] * 4 + [IN_VMEM],
+        in_specs=[IN_HBM] * 5,
         out_specs=(IN_VMEM,) * plan.peers,
-        scratch_shapes=[pltpu.SemaphoreType.DMA(())],
-    )(*arrays, positions)
+        scratch_shapes=[
+            pltpu.VMEM(positions.shape, jnp.int32),
+            pltpu.SemaphoreType.DMA(()),
+            pltpu.SemaphoreType.DMA(()),
+        ],
+        compiler_params=pltpu.CompilerParams(vmem_limit_bytes=6 << 20),
+    )(*(pltpu.with_memory_space_constraint(value, pltpu.HBM) for value in (*arrays, positions)))
 
 
 def selection(rows, columns, shift, limit=None):
@@ -163,28 +172,15 @@
     bufs = refs[1 : 1 + peers]
     outs = refs[1 + peers : 1 + 2 * peers]
     sink_out = refs[1 + 2 * peers]
-    (x_ref, count_ref, y_ref, kt_ref, vt_ref, s_ref, dk_ref, dv_ref, r_ref, sem) = refs[
+    (x_ref, count_ref, y_ref, kt_ref, vt_ref, s_ref, dk_ref, dv_ref, r_ref) = refs[
         2 + 2 * peers :
     ]
-    copies = []
     for k in range(peers):
-        first = plan.first_row(k)
+        first = pl.ds(plan.first_row(k), rows)
         for at in range(4):
-            copies.append(
-                pltpu.make_async_copy(
-                    bufs[k].at[pl.ds(at * rows, rows), :],
-                    x_ref.at[at, pl.ds(first, rows), :],
-                    sem,
-                )
-            )
-        copies.append(
-            pltpu.make_async_copy(
-                bufs[k].at[pl.ds(4 * rows, COUNT_ROWS), :],
-                count_ref.at[pl.ds(plan.first_count(k), COUNT_ROWS), :],
-                sem,
-            )
-        )
-    run_copies(copies)
+            x_ref[at, first, :] = bufs[k][at * rows : (at + 1) * rows, :]
+        first = pl.ds(plan.first_count(k), COUNT_ROWS)
+        count_ref[first, :] = bufs[k][4 * rows :, :]
 
     shard_counts = []
     for shard in range(plan.seq):
@@ -304,24 +300,13 @@
     for slab in range(plan.slabs):
         spread(plan, slab, shard_counts[2 * slab], shard_counts[2 * slab + 1], r_ref, x_ref)
 
-    copies = []
     for k in range(peers):
-        first = plan.first_row(k)
+        first = pl.ds(plan.first_row(k), rows)
         for at in range(4):
-            copies.append(
-                pltpu.make_async_copy(
-                    x_ref.at[at, pl.ds(first, rows), :],
-                    outs[k].at[pl.ds(at * rows, rows), :],
-                    sem,
-                )
-            )
-    for copy in copies:
-        copy.start()
+            outs[k][at * rows : (at + 1) * rows, :] = x_ref[at, first, :]
     total = jnp.sum(sink_sum, axis=1, keepdims=True)
     row = lax.broadcasted_iota(jnp.int32, sink_out.shape, 0)
     sink_out[...] = jnp.where(row == local_head, total, 0.0)
-    for copy in copies:
-        copy.wait()
 
 
 def attention(plan, head, sink_logits, bufs):
@@ -332,8 +317,8 @@
     results = pl.pallas_call(
         functools.partial(attention_kernel, plan, head),
         out_shape=(out,) * plan.peers + (jax.ShapeDtypeStruct((sink_rows, DH), F32),),
-        in_specs=[pl.BlockSpec(memory_space=pltpu.SMEM)] + [ANY] * plan.peers,
-        out_specs=(ANY,) * plan.peers + (IN_VMEM,),
+        in_specs=[pl.BlockSpec(memory_space=pltpu.SMEM)] + [IN_VMEM] * plan.peers,
+        out_specs=(IN_VMEM,) * (plan.peers + 1),
         scratch_shapes=[
             pltpu.VMEM((4, plan.slots, DH), BF16),
             pltpu.VMEM((plan.peers * COUNT_ROWS, DH), BF16),
@@ -344,8 +329,8 @@
             pltpu.VMEM((kept, DH), F32),
             pltpu.VMEM((kept, DH), F32),
             pltpu.VMEM((4, reach, DH), BF16),
-            pltpu.SemaphoreType.DMA(()),
         ],
+        compiler_params=pltpu.CompilerParams(vmem_limit_bytes=24 << 20),
     )(sink_logits, *bufs)
     return results[:-1], results[-1]
 
@@ -379,6 +364,7 @@
         out_specs=(ANY,) * 4,
         scratch_shapes=[pltpu.SemaphoreType.DMA(())],
         input_output_aliases={plan.peers + at: at for at in range(len(held))},
+        compiler_params=pltpu.CompilerParams(vmem_limit_bytes=6 << 20),
     )(*bufs, *held)
 
 

time: 105 us -> 95.4 us (0.909)
  Pallas kernels: 28.8 us -> 15.8 us
  waiting for transfers between devices: 36.2 us -> 45.2 us
  starting transfers between devices: 35.8 us -> 32.7 us
  local copies, waits for them, and re-layouts: 2.07 us -> 0.63 us
    ppermute x28, waiting for transfers between devices: 28.2 us -> 38 us  [exchange(): swapped[k] = lax.ppermute(bufs[k], axes, pairs)]
    pallas_call x2, Pallas kernels: 17.1 us -> 10.7 us  [attention(): pl.pallas_call(functools.partial(attention_kernel, plan, head), out_shape...]
    ppermute x28, starting transfers between devices: 30.9 us -> 27 us  [exchange(): swapped[k] = lax.ppermute(bufs[k], axes, pairs)]
    pallas_call x2, Pallas kernels: 6.5 us -> 2.88 us  [pack(): pl.pallas_call(functools.partial(pack_kernel, plan, head), out_shape=(out...]
    pallas_call x2, Pallas kernels: 5.15 us -> 2.23 us  [unpack(): pl.pallas_call(functools.partial(unpack_kernel, plan, head, carried), out...]
    unnamed x68 -> x2, local copies, waits for them, and re-layouts: 1.44 us -> 0.01 us
  transfers between devices with their start and end apart: 32 -> 32, of which waited for: 15 -> 18; matrix products, arithmetic and copies ran while one was open for 1% -> 1% of each run, Pallas kernels for 22% -> 14%
where the time goes in v1:
time: 95.4 us; the launch traced here: 95.1 us
  waiting for transfers between devices  45.2 us (47%)
  starting transfers between devices  32.7 us (34%)
  Pallas kernels  15.8 us (17%)
    ppermute x28, waiting for transfers between devices, exchange(): swapped[k] = lax.ppermute(bufs[k], axes, pairs)  38 us
    ppermute x28, starting transfers between devices, exchange(): swapped[k] = lax.ppermute(bufs[k], axes, pairs)  27 us
    pallas_call x2, Pallas kernels, attention(): pl.pallas_call(functools.partial(attention_kernel, plan, head), out_shape...  10.7 us
    ppermute x4, waiting for transfers between devices, swap_sum(): return value + lax.ppermute(value, axis, pairs)  7.23 us
    ppermute x4, starting transfers between devices, swap_sum(): return value + lax.ppermute(value, axis, pairs)  5.72 us
    pallas_call x2, Pallas kernels, pack(): pl.pallas_call(functools.partial(pack_kernel, plan, head), out_shape=(out...  2.88 us
    pallas_call x2, Pallas kernels, unpack(): pl.pallas_call(functools.partial(unpack_kernel, plan, head, carried), out...  2.23 us
  transfers between devices with their start and end apart: 32, of which 18 were waited for; matrix products, arithmetic and copies ran while one was open for 1% of the time, Pallas kernels for 14%

profile of v1, /device:TPU:0, one launch (start us, length us, event | category | flops | bytes accessed | tf_op | source)
XLA Modules:
  0.0 95.1 jit_solution(3188693944519022798)
XLA Ops:
  0.6 1.4 %shard_map.103 = (bf16[784,128]{1,0:T(8,128)(2,1)S(1)}, bf16[784,128]{1,0:T(8,128)(2,1)S(1)}, bf16[784,128]{1,0:T(8,128)(2,1)S(1)}, bf16[784,128]{1,0:T(8,128)(2...) custom-call(bf16[1,192,2048]{2,1,0:T(8,128)(2,1)} %refs_0_.6, ...), custom_call_target="tpu_custom_call" | custom-call | tf_op jit(solution)/shard_map/pallas_call | solution.py:103
  2.1 3.1 %collective-permute-start.14 = (bf16[784,128]{1,0:T(8,128)(2,1)S(1)}, bf16[784,128]{1,0:T(8,128)(2,1)S(1)}, u32[]{:S(2)}, u32[]{:S(2)}) collective-permute-start(bf16[784,128]{1,0:T(8,128)(2,1)S(1)} %get-tuple-element.64), channel_id=1, source_target_pairs={{0,1},{1,0},{8,9},{9,8},{16,17},{17,16},{24,25},{25,24},{2,3},{3,2... | collective-permute-start | bytes 602120 | tf_op jit(solution)/shard_map/ppermute | solution.py:377
  5.3 1.9 %collective-permute-start.17 = (bf16[784,128]{1,0:T(8,128)(2,1)S(1)}, bf16[784,128]{1,0:T(8,128)(2,1)S(1)}, u32[]{:S(2)}, u32[]{:S(2)}) collective-permute-start(bf16[784,128]{1,0:T(8,128)(2,1)S(1)} %get-tuple-element.67), channel_id=1, source_target_pairs={{0,16},{1,17},{8,24},{9,25},{16,0},{17,1},{24,8},{25,9},{2,18},{3,... | collective-permute-start | bytes 602120 | tf_op jit(solution)/shard_map/ppermute | solution.py:377
  7.3 1.5 %collective-permute-start.18 = (bf16[784,128]{1,0:T(8,128)(2,1)S(1)}, bf16[784,128]{1,0:T(8,128)(2,1)S(1)}, u32[]{:S(2)}, u32[]{:S(2)}) collective-permute-start(bf16[784,128]{1,0:T(8,128)(2,1)S(1)} %get-tuple-element.68), channel_id=1, source_target_pairs={{0,17},{1,16},{8,25},{9,24},{16,1},{17,0},{24,9},{25,8},{2,19},{3,... | collective-permute-start | bytes 602120 | tf_op jit(solution)/shard_map/ppermute | solution.py:377
  11.0 3.2 %collective-permute-start.20 = (bf16[784,128]{1,0:T(8,128)(2,1)S(1)}, bf16[784,128]{1,0:T(8,128)(2,1)S(1)}, u32[]{:S(2)}, u32[]{:S(2)}) collective-permute-start(bf16[784,128]{1,0:T(8,128)(2,1)S(1)} %get-tuple-element.70), channel_id=1, source_target_pairs={{0,25},{1,24},{8,17},{9,16},{16,9},{17,8},{24,1},{25,0},{2,27},{3,... | collective-permute-start | bytes 602120 | tf_op jit(solution)/shard_map/ppermute | solution.py:377
  14.2 3.8 %collective-permute-done.16.refs_4_ = bf16[784,128]{1,0:T(8,128)(2,1)S(1)} collective-permute-done((bf16[784,128]{1,0:T(8,128)(2,1)S(1)}, bf16[784,128]{1,0:T(8,128)(2,1)S(1)}, u32[]{:S(2)}, u32[]{:S(2)}) %collective-permute-start.16) | collective-permute-done | bytes 200736 | tf_op jit(solution)/shard_map/ppermute | solution.py:377
  22.0 3.7 %collective-permute-done.20.refs_8_ = bf16[784,128]{1,0:T(8,128)(2,1)S(1)} collective-permute-done((bf16[784,128]{1,0:T(8,128)(2,1)S(1)}, bf16[784,128]{1,0:T(8,128)(2,1)S(1)}, u32[]{:S(2)}, u32[]{:S(2)}) %collective-permute-start.20) | collective-permute-done | bytes 200736 | tf_op jit(solution)/shard_map/ppermute | solution.py:377
  27.1 2.9 %collective-permute-done.refs_2_ = bf16[784,128]{1,0:T(8,128)(2,1)S(1)} collective-permute-done((bf16[784,128]{1,0:T(8,128)(2,1)S(1)}, bf16[784,128]{1,0:T(8,128)(2,1)S(1)}, u32[]{:S(2)}, u32[]{:S(2)}) %collective-permute-start) | collective-permute-done | bytes 200736 | tf_op jit(solution)/shard_map/ppermute | solution.py:377
  32.1 5.3 %shard_map.104 = (bf16[768,128]{1,0:T(8,128)(2,1)S(1)}, bf16[768,128]{1,0:T(8,128)(2,1)S(1)}, bf16[768,128]{1,0:T(8,128)(2,1)S(1)}, bf16[768,128]{1,0:T(8,128)(2...) custom-call(f32[8]{0:T(128)S(1)} %copy-done, ...), custom_call_target="tpu_custom_call" | custom-call | tf_op jit(solution)/shard_map/pallas_call | solution.py:317
  40.7 1.6 %collective-permute-start.24 = (bf16[768,128]{1,0:T(8,128)(2,1)S(1)}, bf16[768,128]{1,0:T(8,128)(2,1)S(1)}, u32[]{:S(2)}, u32[]{:S(2)}) collective-permute-start(bf16[768,128]{1,0:T(8,128)(2,1)S(1)} %get-tuple-element.75), channel_id=1, source_target_pairs={{0,16},{1,17},{8,24},{9,25},{16,0},{17,1},{24,8},{25,9},{2,18},{3,... | collective-permute-start | bytes 589832 | tf_op jit(solution)/shard_map/ppermute | solution.py:377
  43.6 5.3 %shard_map.102 = (bf16[768,128]{1,0:T(8,128)(2,1)S(1)}, bf16[768,128]{1,0:T(8,128)(2,1)S(1)}, bf16[768,128]{1,0:T(8,128)(2,1)S(1)}, bf16[768,128]{1,0:T(8,128)(2...) custom-call(f32[8]{0:T(128)S(1)} %copy-done, ...), custom_call_target="tpu_custom_call" | custom-call | tf_op jit(solution)/shard_map/pallas_call | solution.py:317
  49.0 1.6 %collective-permute-start.28 = (f32[8,128]{1,0:T(8,128)S(1)}, f32[8,128]{1,0:T(8,128)S(1)}, u32[]{:S(2)}, u32[]{:S(2)}) collective-permute-start(f32[8,128]{1,0:T(8,128)S(1)} %add.15), channel_id=1, source_target_pairs={{0,16},{8,24},{16,0},{24,8},{1,17},{9,25},{17,1},{25,9},{2,18},{10... | collective-permute-start | bytes 12296 | tf_op jit(solution)/shard_map/ppermute | solution.py:383
  50.6 2.1 %collective-permute-done.28 = f32[8,128]{1,0:T(8,128)S(1)} collective-permute-done((f32[8,128]{1,0:T(8,128)S(1)}, f32[8,128]{1,0:T(8,128)S(1)}, u32[]{:S(2)}, u32[]{:S(2)}) %collective-permute-start.28) | collective-permute-done | bytes 4128 | tf_op jit(solution)/shard_map/ppermute | solution.py:383
  53.9 2.6 %collective-permute-start.30 = (f32[8,128]{1,0:T(8,128)S(1)}, f32[8,128]{1,0:T(8,128)S(1)}, u32[]{:S(2)}, u32[]{:S(2)}) collective-permute-start(f32[8,128]{1,0:T(8,128)S(1)} %add.17), channel_id=1, source_target_pairs={{0,4},{2,6},{4,0},{6,2},{1,5},{3,7},{5,1},{7,3},{8,12},{10,14},{12... | collective-permute-start | bytes 12296 | tf_op jit(solution)/shard_map/ppermute | solution.py:383
  56.4 1.9 %collective-permute-done.30 = f32[8,128]{1,0:T(8,128)S(1)} collective-permute-done((f32[8,128]{1,0:T(8,128)S(1)}, f32[8,128]{1,0:T(8,128)S(1)}, u32[]{:S(2)}, u32[]{:S(2)}) %collective-permute-start.30) | collective-permute-done | bytes 4128 | tf_op jit(solution)/shard_map/ppermute | solution.py:383
  58.4 1.6 %collective-permute-start.31 = (f32[8,128]{1,0:T(8,128)S(1)}, f32[8,128]{1,0:T(8,128)S(1)}, u32[]{:S(2)}, u32[]{:S(2)}) collective-permute-start(f32[8,128]{1,0:T(8,128)S(1)} %add.18), channel_id=1, source_target_pairs={{0,2},{2,0},{4,6},{6,4},{1,3},{3,1},{5,7},{7,5},{8,10},{10,8},{12,... | collective-permute-start | bytes 12296 | tf_op jit(solution)/shard_map/ppermute | solution.py:383
  59.9 2.0 %collective-permute-done.31 = f32[8,128]{1,0:T(8,128)S(1)} collective-permute-done((f32[8,128]{1,0:T(8,128)S(1)}, f32[8,128]{1,0:T(8,128)S(1)}, u32[]{:S(2)}, u32[]{:S(2)}) %collective-permute-start.31) | collective-permute-done | bytes 4128 | tf_op jit(solution)/shard_map/ppermute | solution.py:383
  63.4 2.7 %collective-permute-start.27 = (bf16[768,128]{1,0:T(8,128)(2,1)S(1)}, bf16[768,128]{1,0:T(8,128)(2,1)S(1)}, u32[]{:S(2)}, u32[]{:S(2)}) collective-permute-start(bf16[768,128]{1,0:T(8,128)(2,1)S(1)} %get-tuple-element.78), channel_id=1, source_target_pairs={{0,25},{1,24},{8,17},{9,16},{16,9},{17,8},{24,1},{25,0},{2,27},{3,... | collective-permute-start | bytes 589832 | tf_op jit(solution)/shard_map/ppermute | solution.py:377
  66.6 3.1 %collective-permute-done.25.refs_5_ = bf16[768,128]{1,0:T(8,128)(2,1)S(1)} collective-permute-done((bf16[768,128]{1,0:T(8,128)(2,1)S(1)}, bf16[768,128]{1,0:T(8,128)(2,1)S(1)}, u32[]{:S(2)}, u32[]{:S(2)}) %collective-permute-start.25) | collective-permute-done | bytes 196640 | tf_op jit(solution)/shard_map/ppermute | solution.py:377
  69.7 3.0 %collective-permute-done.26.refs_6_ = bf16[768,128]{1,0:T(8,128)(2,1)S(1)} collective-permute-done((bf16[768,128]{1,0:T(8,128)(2,1)S(1)}, bf16[768,128]{1,0:T(8,128)(2,1)S(1)}, u32[]{:S(2)}, u32[]{:S(2)}) %collective-permute-start.26) | collective-permute-done | bytes 196640 | tf_op jit(solution)/shard_map/ppermute | solution.py:377
  72.8 3.1 %collective-permute-done.27.refs_7_ = bf16[768,128]{1,0:T(8,128)(2,1)S(1)} collective-permute-done((bf16[768,128]{1,0:T(8,128)(2,1)S(1)}, bf16[768,128]{1,0:T(8,128)(2,1)S(1)}, u32[]{:S(2)}, u32[]{:S(2)}) %collective-permute-start.27) | collective-permute-done | bytes 196640 | tf_op jit(solution)/shard_map/ppermute | solution.py:377
  81.2 4.7 %collective-permute-done.11.refs_5_ = bf16[768,128]{1,0:T(8,128)(2,1)S(1)} collective-permute-done((bf16[768,128]{1,0:T(8,128)(2,1)S(1)}, bf16[768,128]{1,0:T(8,128)(2,1)S(1)}, u32[]{:S(2)}, u32[]{:S(2)}) %collective-permute-start.11) | collective-permute-done | bytes 196640 | tf_op jit(solution)/shard_map/ppermute | solution.py:377
  85.9 2.9 %collective-permute-done.12.refs_6_ = bf16[768,128]{1,0:T(8,128)(2,1)S(1)} collective-permute-done((bf16[768,128]{1,0:T(8,128)(2,1)S(1)}, bf16[768,128]{1,0:T(8,128)(2,1)S(1)}, u32[]{:S(2)}, u32[]{:S(2)}) %collective-permute-start.12) | collective-permute-done | bytes 196640 | tf_op jit(solution)/shard_map/ppermute | solution.py:377
  88.7 5.3 %collective-permute-done.13.refs_7_ = bf16[768,128]{1,0:T(8,128)(2,1)S(1)} collective-permute-done((bf16[768,128]{1,0:T(8,128)(2,1)S(1)}, bf16[768,128]{1,0:T(8,128)(2,1)S(1)}, u32[]{:S(2)}, u32[]{:S(2)}) %collective-permute-start.13) | collective-permute-done | bytes 196640 | tf_op jit(solution)/shard_map/ppermute | solution.py:377
  (54 shorter events, 24.0 us)
Async XLA Ops:
  5.2 12.8 %collective-permute-start.16 = (bf16[784,128]{1,0:T(8,128)(2,1)S(1)}, bf16[784,128]{1,0:T(8,128)(2,1)S(1)}, u32[]{:S(2)}, u32[]{:S(2)}) collective-permute-start(bf16[784,128]{1,0:T(8,128)(2,1)S(1)} %get-tuple-element.66), channel_id=1, source_target_pairs={{0,9},{1,8},{8,1},{9,0},{16,25},{17,24},{24,17},{25,16},{2,11},{3,... | collective-permute-start | bytes 602120 | tf_op jit(solution)/shard_map/ppermute | solution.py:377
  5.3 14.0 %collective-permute-start.17 = (bf16[784,128]{1,0:T(8,128)(2,1)S(1)}, bf16[784,128]{1,0:T(8,128)(2,1)S(1)}, u32[]{:S(2)}, u32[]{:S(2)}) collective-permute-start(bf16[784,128]{1,0:T(8,128)(2,1)S(1)} %get-tuple-element.67), channel_id=1, source_target_pairs={{0,16},{1,17},{8,24},{9,25},{16,0},{17,1},{24,8},{25,9},{2,18},{3,... | collective-permute-start | bytes 602120 | tf_op jit(solution)/shard_map/ppermute | solution.py:377
  7.3 13.1 %collective-permute-start.18 = (bf16[784,128]{1,0:T(8,128)(2,1)S(1)}, bf16[784,128]{1,0:T(8,128)(2,1)S(1)}, u32[]{:S(2)}, u32[]{:S(2)}) collective-permute-start(bf16[784,128]{1,0:T(8,128)(2,1)S(1)} %get-tuple-element.68), channel_id=1, source_target_pairs={{0,17},{1,16},{8,25},{9,24},{16,1},{17,0},{24,9},{25,8},{2,19},{3,... | collective-permute-start | bytes 602120 | tf_op jit(solution)/shard_map/ppermute | solution.py:377
  11.0 10.3 %collective-permute-start.19 = (bf16[784,128]{1,0:T(8,128)(2,1)S(1)}, bf16[784,128]{1,0:T(8,128)(2,1)S(1)}, u32[]{:S(2)}, u32[]{:S(2)}) collective-permute-start(bf16[784,128]{1,0:T(8,128)(2,1)S(1)} %get-tuple-element.69), channel_id=1, source_target_pairs={{0,24},{1,25},{8,16},{9,17},{16,8},{17,9},{24,0},{25,1},{2,26},{3,... | collective-permute-start | bytes 602120 | tf_op jit(solution)/shard_map/ppermute | solution.py:377
  11.0 14.7 %collective-permute-start.20 = (bf16[784,128]{1,0:T(8,128)(2,1)S(1)}, bf16[784,128]{1,0:T(8,128)(2,1)S(1)}, u32[]{:S(2)}, u32[]{:S(2)}) collective-permute-start(bf16[784,128]{1,0:T(8,128)(2,1)S(1)} %get-tuple-element.70), channel_id=1, source_target_pairs={{0,25},{1,24},{8,17},{9,16},{16,9},{17,8},{24,1},{25,0},{2,27},{3,... | collective-permute-start | bytes 602120 | tf_op jit(solution)/shard_map/ppermute | solution.py:377
  18.0 12.0 %collective-permute-start = (bf16[784,128]{1,0:T(8,128)(2,1)S(1)}, bf16[784,128]{1,0:T(8,128)(2,1)S(1)}, u32[]{:S(2)}, u32[]{:S(2)}) collective-permute-start(bf16[784,128]{1,0:T(8,128)(2,1)S(1)} %get-tuple-element.48), channel_id=1, source_target_pairs={{0,1},{1,0},{8,9},{9,8},{16,17},{17,16},{24,25},{25,24},{2,3},{3,2... | collective-permute-start | bytes 602120 | tf_op jit(solution)/shard_map/ppermute | solution.py:377
  19.3 12.0 %collective-permute-start.1 = (bf16[784,128]{1,0:T(8,128)(2,1)S(1)}, bf16[784,128]{1,0:T(8,128)(2,1)S(1)}, u32[]{:S(2)}, u32[]{:S(2)}) collective-permute-start(bf16[784,128]{1,0:T(8,128)(2,1)S(1)} %get-tuple-element.49), channel_id=1, source_target_pairs={{0,8},{1,9},{8,0},{9,1},{16,24},{17,25},{24,16},{25,17},{2,10},{3,... | collective-permute-start | bytes 602120 | tf_op jit(solution)/shard_map/ppermute | solution.py:377
  20.3 18.2 %collective-permute-start.2 = (bf16[784,128]{1,0:T(8,128)(2,1)S(1)}, bf16[784,128]{1,0:T(8,128)(2,1)S(1)}, u32[]{:S(2)}, u32[]{:S(2)}) collective-permute-start(bf16[784,128]{1,0:T(8,128)(2,1)S(1)} %get-tuple-element.50), channel_id=1, source_target_pairs={{0,9},{1,8},{8,1},{9,0},{16,25},{17,24},{24,17},{25,16},{2,11},{3,... | collective-permute-start | bytes 602120 | tf_op jit(solution)/shard_map/ppermute | solution.py:377
  21.3 18.4 %collective-permute-start.3 = (bf16[784,128]{1,0:T(8,128)(2,1)S(1)}, bf16[784,128]{1,0:T(8,128)(2,1)S(1)}, u32[]{:S(2)}, u32[]{:S(2)}) collective-permute-start(bf16[784,128]{1,0:T(8,128)(2,1)S(1)} %get-tuple-element.51), channel_id=1, source_target_pairs={{0,16},{1,17},{8,24},{9,25},{16,0},{17,1},{24,8},{25,9},{2,18},{3,... | collective-permute-start | bytes 602120 | tf_op jit(solution)/shard_map/ppermute | solution.py:377
  25.7 14.0 %collective-permute-start.4 = (bf16[784,128]{1,0:T(8,128)(2,1)S(1)}, bf16[784,128]{1,0:T(8,128)(2,1)S(1)}, u32[]{:S(2)}, u32[]{:S(2)}) collective-permute-start(bf16[784,128]{1,0:T(8,128)(2,1)S(1)} %get-tuple-element.52), channel_id=1, source_target_pairs={{0,17},{1,16},{8,25},{9,24},{16,1},{17,0},{24,9},{25,8},{2,19},{3,... | collective-permute-start | bytes 602120 | tf_op jit(solution)/shard_map/ppermute | solution.py:377
  30.0 10.6 %collective-permute-start.5 = (bf16[784,128]{1,0:T(8,128)(2,1)S(1)}, bf16[784,128]{1,0:T(8,128)(2,1)S(1)}, u32[]{:S(2)}, u32[]{:S(2)}) collective-permute-start(bf16[784,128]{1,0:T(8,128)(2,1)S(1)} %get-tuple-element.53), channel_id=1, source_target_pairs={{0,24},{1,25},{8,16},{9,17},{16,8},{17,9},{24,0},{25,1},{2,26},{3,... | collective-permute-start | bytes 602120 | tf_op jit(solution)/shard_map/ppermute | solution.py:377
  31.3 12.3 %collective-permute-start.6 = (bf16[784,128]{1,0:T(8,128)(2,1)S(1)}, bf16[784,128]{1,0:T(8,128)(2,1)S(1)}, u32[]{:S(2)}, u32[]{:S(2)}) collective-permute-start(bf16[784,128]{1,0:T(8,128)(2,1)S(1)} %get-tuple-element.54), channel_id=1, source_target_pairs={{0,25},{1,24},{8,17},{9,16},{16,9},{17,8},{24,1},{25,0},{2,27},{3,... | collective-permute-start | bytes 602120 | tf_op jit(solution)/shard_map/ppermute | solution.py:377
  38.5 24.9 %collective-permute-start.21 = (bf16[768,128]{1,0:T(8,128)(2,1)S(1)}, bf16[768,128]{1,0:T(8,128)(2,1)S(1)}, u32[]{:S(2)}, u32[]{:S(2)}) collective-permute-start(bf16[768,128]{1,0:T(8,128)(2,1)S(1)} %get-tuple-element.72), channel_id=1, source_target_pairs={{0,1},{1,0},{8,9},{9,8},{16,17},{17,16},{24,25},{25,24},{2,3},{3,2... | collective-permute-start | bytes 589832 | tf_op jit(solution)/shard_map/ppermute | solution.py:377
  39.7 23.7 %collective-permute-start.22 = (bf16[768,128]{1,0:T(8,128)(2,1)S(1)}, bf16[768,128]{1,0:T(8,128)(2,1)S(1)}, u32[]{:S(2)}, u32[]{:S(2)}) collective-permute-start(bf16[768,128]{1,0:T(8,128)(2,1)S(1)} %get-tuple-element.73), channel_id=1, source_target_pairs={{0,8},{1,9},{8,0},{9,1},{16,24},{17,25},{24,16},{25,17},{2,10},{3,... | collective-permute-start | bytes 589832 | tf_op jit(solution)/shard_map/ppermute | solution.py:377
  39.7 26.4 %collective-permute-start.23 = (bf16[768,128]{1,0:T(8,128)(2,1)S(1)}, bf16[768,128]{1,0:T(8,128)(2,1)S(1)}, u32[]{:S(2)}, u32[]{:S(2)}) collective-permute-start(bf16[768,128]{1,0:T(8,128)(2,1)S(1)} %get-tuple-element.74), channel_id=1, source_target_pairs={{0,9},{1,8},{8,1},{9,0},{16,25},{17,24},{24,17},{25,16},{2,11},{3,... | collective-permute-start | bytes 589832 | tf_op jit(solution)/shard_map/ppermute | solution.py:377
  40.7 26.0 %collective-permute-start.24 = (bf16[768,128]{1,0:T(8,128)(2,1)S(1)}, bf16[768,128]{1,0:T(8,128)(2,1)S(1)}, u32[]{:S(2)}, u32[]{:S(2)}) collective-permute-start(bf16[768,128]{1,0:T(8,128)(2,1)S(1)} %get-tuple-element.75), channel_id=1, source_target_pairs={{0,16},{1,17},{8,24},{9,25},{16,0},{17,1},{24,8},{25,9},{2,18},{3,... | collective-permute-start | bytes 589832 | tf_op jit(solution)/shard_map/ppermute | solution.py:377
  63.4 9.3 %collective-permute-start.26 = (bf16[768,128]{1,0:T(8,128)(2,1)S(1)}, bf16[768,128]{1,0:T(8,128)(2,1)S(1)}, u32[]{:S(2)}, u32[]{:S(2)}) collective-permute-start(bf16[768,128]{1,0:T(8,128)(2,1)S(1)} %get-tuple-element.77), channel_id=1, source_target_pairs={{0,24},{1,25},{8,16},{9,17},{16,8},{17,9},{24,0},{25,1},{2,26},{3,... | collective-permute-start | bytes 589832 | tf_op jit(solution)/shard_map/ppermute | solution.py:377
  63.4 12.5 %collective-permute-start.27 = (bf16[768,128]{1,0:T(8,128)(2,1)S(1)}, bf16[768,128]{1,0:T(8,128)(2,1)S(1)}, u32[]{:S(2)}, u32[]{:S(2)}) collective-permute-start(bf16[768,128]{1,0:T(8,128)(2,1)S(1)} %get-tuple-element.78), channel_id=1, source_target_pairs={{0,25},{1,24},{8,17},{9,16},{16,9},{17,8},{24,1},{25,0},{2,27},{3,... | collective-permute-start | bytes 589832 | tf_op jit(solution)/shard_map/ppermute | solution.py:377
  66.1 11.8 %collective-permute-start.7 = (bf16[768,128]{1,0:T(8,128)(2,1)S(1)}, bf16[768,128]{1,0:T(8,128)(2,1)S(1)}, u32[]{:S(2)}, u32[]{:S(2)}) collective-permute-start(bf16[768,128]{1,0:T(8,128)(2,1)S(1)} %get-tuple-element.56), channel_id=1, source_target_pairs={{0,1},{1,0},{8,9},{9,8},{16,17},{17,16},{24,25},{25,24},{2,3},{3,2... | collective-permute-start | bytes 589832 | tf_op jit(solution)/shard_map/ppermute | solution.py:377
  66.6 11.7 %collective-permute-start.8 = (bf16[768,128]{1,0:T(8,128)(2,1)S(1)}, bf16[768,128]{1,0:T(8,128)(2,1)S(1)}, u32[]{:S(2)}, u32[]{:S(2)}) collective-permute-start(bf16[768,128]{1,0:T(8,128)(2,1)S(1)} %get-tuple-element.57), channel_id=1, source_target_pairs={{0,8},{1,9},{8,0},{9,1},{16,24},{17,25},{24,16},{25,17},{2,10},{3,... | collective-permute-start | bytes 589832 | tf_op jit(solution)/shard_map/ppermute | solution.py:377
  69.7 11.4 %collective-permute-start.9 = (bf16[768,128]{1,0:T(8,128)(2,1)S(1)}, bf16[768,128]{1,0:T(8,128)(2,1)S(1)}, u32[]{:S(2)}, u32[]{:S(2)}) collective-permute-start(bf16[768,128]{1,0:T(8,128)(2,1)S(1)} %get-tuple-element.58), channel_id=1, source_target_pairs={{0,9},{1,8},{8,1},{9,0},{16,25},{17,24},{24,17},{25,16},{2,11},{3,... | collective-permute-start | bytes 589832 | tf_op jit(solution)/shard_map/ppermute | solution.py:377
  75.9 10.0 %collective-permute-start.11 = (bf16[768,128]{1,0:T(8,128)(2,1)S(1)}, bf16[768,128]{1,0:T(8,128)(2,1)S(1)}, u32[]{:S(2)}, u32[]{:S(2)}) collective-permute-start(bf16[768,128]{1,0:T(8,128)(2,1)S(1)} %get-tuple-element.60), channel_id=1, source_target_pairs={{0,17},{1,16},{8,25},{9,24},{16,1},{17,0},{24,9},{25,8},{2,19},{3,... | collective-permute-start | bytes 589832 | tf_op jit(solution)/shard_map/ppermute | solution.py:377
  77.9 10.8 %collective-permute-start.12 = (bf16[768,128]{1,0:T(8,128)(2,1)S(1)}, bf16[768,128]{1,0:T(8,128)(2,1)S(1)}, u32[]{:S(2)}, u32[]{:S(2)}) collective-permute-start(bf16[768,128]{1,0:T(8,128)(2,1)S(1)} %get-tuple-element.61), channel_id=1, source_target_pairs={{0,24},{1,25},{8,16},{9,17},{16,8},{17,9},{24,0},{25,1},{2,26},{3,... | collective-permute-start | bytes 589832 | tf_op jit(solution)/shard_map/ppermute | solution.py:377
  78.3 15.7 %collective-permute-start.13 = (bf16[768,128]{1,0:T(8,128)(2,1)S(1)}, bf16[768,128]{1,0:T(8,128)(2,1)S(1)}, u32[]{:S(2)}, u32[]{:S(2)}) collective-permute-start(bf16[768,128]{1,0:T(8,128)(2,1)S(1)} %get-tuple-element.62), channel_id=1, source_target_pairs={{0,25},{1,24},{8,17},{9,16},{16,9},{17,8},{24,1},{25,0},{2,27},{3,... | collective-permute-start | bytes 589832 | tf_op jit(solution)/shard_map/ppermute | solution.py:377
  (9 other events, 44.7 us)
